TPU v7x, 32 devices: a whole 2x2x4 slice. The times are simulated.
32 devices in a mesh: pts: 8 (over z, y), feat: 4 (over x, core).
Axes of the slice: x: 2, y: 2, z: 4, core: 2. Of those that a mesh axis runs over, the one named last changes fastest.
Arguments:
- slab: bfloat16 [16384, 768], P('pts', 'feat'), may hold values from -40 to 40
- centres: bfloat16 [4096, 768], replicated, may hold values from -3 to 3
- labels: int32 [16384, 1], P(('pts', 'feat')), may hold values from 0 to 4095
- sample_rows: int32 [8, 8, 4], P('pts'), may hold values from 0 to 2047, as said below
- sample_count: int32 [8, 8], P('pts'), may hold values from 0 to 4, as said below
- slot_offset: int32 [8, 8], P('pts'), may hold values from 0 to 28, as said below
Outputs:
- coreset: bfloat16 [256, 768], P('pts', 'feat')
Inputs may be any that keep to these rules, and one draw needn't show every extreme that they name: `sample_rows`: row indices within a source shard; sampled independently with replacement. `sample_count`: in every draw some owner receives 4 rows from every source. slot_offset[o,p] is the sum of sample_count[q,o] over sources q < p.
All inputs are finite; a program needn't handle non-finite values.
Results may differ from a plain program's by a relative error of at most 0.0006.
Values may be sent and summed in bfloat16 or wider, within the bound.
A program may use at most 64 MiB of HBM per device.

v0:
```python
import jax
import jax.numpy as jnp
from jax import lax
from jax.sharding import PartitionSpec as P


def local(slab, centres, labels, sample_rows, sample_count, slot_offset):
    rows_pts, feat_width = slab.shape
    feat_count = lax.axis_size("feat")
    rows_dev = rows_pts // feat_count
    centre_count = centres.shape[0]
    contract = (((1,), (1,)), ((), ()))
    centre_sq = jnp.sum(jnp.square(centres.astype(jnp.float32)), axis=1)
    stacked = slab.reshape(feat_count, rows_dev, feat_width)
    points = lax.all_to_all(stacked, "feat", split_axis=0, concat_axis=2, tiled=True)[0]
    cross_term = lax.dot_general(points, centres, contract, preferred_element_type=jnp.float32)
    point_sq = jnp.sum(jnp.square(points.astype(jnp.float32)), axis=1)
    nearest = jnp.min(point_sq[:, None] + centre_sq[None, :] - 2.0 * cross_term, axis=1)[None, :][0]
    member = labels[:, 0]
    cost_part = jax.ops.segment_sum(nearest, member, num_segments=centre_count)
    size_part = jax.ops.segment_sum(jnp.ones_like(nearest), member, num_segments=centre_count)
    cluster_cost, cluster_size = lax.psum((cost_part, size_part), ("pts", "feat"))
    own_sens = nearest / jnp.take(cluster_cost, member) + 1.0 / jnp.take(cluster_size, member)
    shard_sens = lax.all_gather(own_sens, "feat", axis=0, tiled=True)
    total_points = rows_pts * lax.axis_size("pts")
    weight = 2.0 * centre_count / total_points / shard_sens
    picked_rows = sample_rows[0]
    owner_count, slot_count = picked_rows.shape
    chosen = jnp.take(slab, picked_rows.reshape(-1), axis=0).reshape(
        owner_count, slot_count, feat_width
    )
    chosen_weight = jnp.take(weight, picked_rows)
    live_slot = jnp.arange(slot_count, dtype=jnp.int32)[None, :] < sample_count[0][:, None]
    scaled = jnp.where(
        live_slot[:, :, None], chosen.astype(jnp.float32) * chosen_weight[:, :, None], 0.0
    ).astype(jnp.bfloat16)
    arrived = lax.all_to_all(scaled, "pts", split_axis=0, concat_axis=0, tiled=True)
    target = slot_offset[0][:, None] + jnp.arange(slot_count, dtype=jnp.int32)[None, :]
    own_rows = arrived.shape[0] * slot_count
    placed = jnp.zeros((own_rows, feat_width), jnp.float32)
    placed = placed.at[target.reshape(-1)].add(
        arrived.reshape(-1, feat_width).astype(jnp.float32), mode="drop"
    )
    return placed.astype(jnp.bfloat16)


def solution(mesh):
    placed = (
        P("pts", "feat"),
        P(),
        P(("pts", "feat"), None),
        P("pts", None, None),
        P("pts", None),
        P("pts", None),
    )
    return jax.shard_map(
        local, mesh=mesh, in_specs=placed, out_specs=P("pts", "feat"), check_vma=False
    )
```

profile of v0, /device:TPU:0, one launch (start us, length us, event | category | flops | bytes accessed | tf_op | source)
XLA Modules:
  0.0 99.5 jit_solution(1397401444950790253)
XLA Ops:
  0.0 2.1 %copy.35 = bf16[24,4,8,512]{3,2,0,1:T(8,128)(2,1)} copy(bf16[24,4,8,512]{3,2,1,0:T(8,128)(2,1)} %bitcast.31) | data formatting | bytes 1572864 | tf_op jit(solution)/shard_map/reshape | solution.py:14
  2.1 4.2 %all-to-all-start = ((bf16[4,512,192]{1,2,0:T(8,128)(2,1)}), bf16[4,512,192]{1,2,0:T(8,128)(2,1)S(1)}, u32[]{:S(2)}, u32[]{:S(2)}) async-start(bf16[4,512,192]{1,2,0:T(8,128)(2,1)} %bitcast.29), calls=%async_computation | async-start | bytes 1572864 | tf_op jit(solution)/shard_map/all_to_all | solution.py:15
  6.3 1.4 %copy.28 = bf16[2048,192]{1,0:T(8,128)(2,1)S(1)} copy(bf16[2048,192]{0,1:T(8,128)(2,1)} %param.8) | data formatting | bytes 1572864 | tf_op args[0]
  7.8 0.7 compare_select_fusion.1
  8.4 0.8 copy.27
  9.2 0.7 compare_select_fusion
  10.2 0.6 gather_fusion
  10.8 0.7 iota_compare_fusion
  11.5 0.7 iota_add_fusion
  12.3 3.4 %scatter_custom_fusion.1 = f32[4096]{0:T(1024)S(1)} fusion(s32[512]{0:T(512)} %bitcast.35, f32[512]{0:T(512)S(1)} %broadcast.113, f32[]{:T(128)} %constant.22.clone.1), kind=kCustom, calls=%fused_computation.14 | custom fusion | flops 512 | bytes 16896 | tf_op jit(solution)/shard_map/scatter-add | solution.py:21
  15.8 4.1 %multiply_reduce_fusion = f32[4096]{0:T(1024)S(1)} fusion(bf16[4096,768]{1,0:T(8,128)(2,1)} %param.9), kind=kLoop, calls=%fused_computation.7 | loop fusion | flops 9433088 | bytes 6307840 | tf_op jit(solution)/shard_map/reduce_sum | solution.py:13
  19.9 0.2 multiply_reduce_fusion.1
  20.1 7.5 %subtract_reduce_fusion = f32[512]{0:T(512)S(1)} fusion(bf16[512,768]{0,1:T(8,128)(2,1)S(1)} %bitcast.32, bf16[4096,768]{1,0:T(8,128)(2,1)} %param.9, f32[4096]{0:T(1024)S(1)} %multiply_reduce_fusion, f32[512]{0:T(512)S(1)} %multiply_reduce_fusion.1), kind=kOutput, calls=%fused_computation.8 | convolution fusion | flops 3229613568 | bytes 7098368 | tf_op jit(solution)/shard_map/dot_general | solution.py:16
  27.6 3.3 %scatter_custom_fusion = f32[4096]{0:T(1024)S(1)} fusion(s32[512]{0:T(512)S(1)} %bitcast.36, f32[512]{0:T(512)S(1)} %subtract_reduce_fusion, f32[]{:T(128)} %constant.22.clone.1), kind=kCustom, calls=%fused_computation.16 | custom fusion | flops 512 | bytes 16388 | tf_op jit(solution)/shard_map/scatter-add | solution.py:20
  30.9 42.0 %all-reduce = (f32[4096]{0:T(1024)S(1)}, f32[4096]{0:T(1024)S(1)}) all-reduce(f32[4096]{0:T(1024)S(1)} %scatter_custom_fusion.1, f32[4096]{0:T(1024)S(1)} %scatter_custom_fusion), channel_id=1, replica_groups=mesh['pts'=8,'feat'=4] {'pts','feat'}, use_global_device_ids=true, to_apply=%region_6.8 | all-reduce | flops 8192 | bytes 65536 | tf_op jit(solution)/shard_map/psum | solution.py:22
  72.9 3.1 %gather_fusion.2 = f32[512]{0:T(512)S(1)} fusion(f32[4096]{0:T(1024)S(1)} %get-tuple-element.7, s32[1024]{0:T(1024)S(1)} %pad_clamp_fusion.1), kind=kCustom, calls=%fused_computation.clone | custom fusion | bytes 6144 | tf_op jit(solution)/shard_map/jit(_take)/gather | solution.py:23
  76.0 3.1 %gather_fusion.3 = f32[512]{0:T(512)S(1)} fusion(f32[4096]{0:T(1024)S(1)} %get-tuple-element.6, s32[1024]{0:T(1024)S(1)} %pad_clamp_fusion.1), kind=kCustom, calls=%fused_computation.1.clone | custom fusion | bytes 6144 | tf_op jit(solution)/shard_map/jit(_take)/gather | solution.py:23
  79.2 5.5 %all-gather = f32[4,1,512]{2,1,0:T(1,128)S(1)} all-gather(f32[1,1,512]{2,1,0:T(1,128)S(1)} %bitcast.33), channel_id=1, replica_groups=mesh['pts'=8,'feat'=4] {'feat'}, dimensions={0}, use_global_device_ids=true | all-gather | bytes 10240 | tf_op jit(solution)/shard_map/all_gather | solution.py:24
  84.7 0.7 gather_fusion.1
  85.7 0.7 select_convert_fusion
  86.4 5.1 %all-to-all-start.1 = ((bf16[8,4,192]{2,1,0:T(4,128)(2,1)}), bf16[8,4,192]{2,1,0:T(4,128)(2,1)S(1)}, u32[]{:S(2)}, u32[]{:S(2)}) async-start(bf16[8,4,192]{2,1,0:T(4,128)(2,1)} %select_convert_fusion), calls=%async_computation.1 | async-start | bytes 32768 | tf_op jit(solution)/shard_map/all_to_all | solution.py:37
  91.5 6.6 %all-to-all-done.1 = bf16[8,4,192]{2,1,0:T(4,128)(2,1)S(1)} async-done(((bf16[8,4,192]{2,1,0:T(4,128)(2,1)}), bf16[8,4,192]{2,1,0:T(4,128)(2,1)S(1)}, u32[]{:S(2)}, u32[]{:S(2)}) %all-to-all-start.1) | async-done | bytes 12320 | tf_op jit(solution)/shard_map/all_to_all | solution.py:37
  98.1 0.8 scatter_custom_fusion.2
  98.9 0.6 convert_element_type.28
  (24 shorter events, 0.8 us)
Async XLA Ops:
  2.1 17.8 %all-to-all-start = ((bf16[4,512,192]{1,2,0:T(8,128)(2,1)}), bf16[4,512,192]{1,2,0:T(8,128)(2,1)S(1)}, u32[]{:S(2)}, u32[]{:S(2)}) async-start(bf16[4,512,192]{1,2,0:T(8,128)(2,1)} %bitcast.29), calls=%async_computation | async-start | bytes 1572864 | tf_op jit(solution)/shard_map/all_to_all | solution.py:15
  20.1 7.5 %copy-start.1 = (s32[512,1]{0,1:T(1,128)S(1)}, s32[512,1]{0,1:T(1,128)}, u32[]{:S(2)}) copy-start(s32[512,1]{0,1:T(1,128)} %param.10) | copy-start | bytes 6148
  27.6 57.9 %copy-start = (s32[1,8,4]{1,2,0:T(4,128)S(1)}, s32[1,8,4]{1,2,0:T(4,128)}, u32[]{:S(2)}) copy-start(s32[1,8,4]{1,2,0:T(4,128)} %param.11) | copy-start | bytes 388
  86.4 11.6 %all-to-all-start.1 = ((bf16[8,4,192]{2,1,0:T(4,128)(2,1)}), bf16[8,4,192]{2,1,0:T(4,128)(2,1)S(1)}, u32[]{:S(2)}, u32[]{:S(2)}) async-start(bf16[8,4,192]{2,1,0:T(4,128)(2,1)} %select_convert_fusion), calls=%async_computation.1 | async-start | bytes 32768 | tf_op jit(solution)/shard_map/all_to_all | solution.py:37
where the time goes:
time: 100 us; the launch traced here: 99.5 us
  blocking collectives  47.4 us (47%)
  other arithmetic  15.9 us (16%)
  local copies, waits for them, and re-layouts  12.6 us (13%)
  starting transfers between devices  9.3 us (9%)
  matrix products  7.52 us (8%)
  waiting for transfers between devices  6.57 us (7%)
    psum x1, blocking collectives, local(): lax.psum((cost_part, size_part), ('pts', 'feat'))  42 us
    dot_general x1, matrix products, local(): lax.dot_general(points, centres, contract, preferred_element_type=jnp.flo...  7.52 us
    all_to_all x1, waiting for transfers between devices, local(): lax.all_to_all(scaled, 'pts', split_axis=0, concat_axis=0, tiled=True)  6.57 us
    all_gather x1, blocking collectives, local(): shard_sens = lax.all_gather(own_sens, 'feat', axis=0, tiled=True)  5.45 us
    all_to_all x1, starting transfers between devices, local(): lax.all_to_all(scaled, 'pts', split_axis=0, concat_axis=0, tiled=True)  5.07 us
    all_to_all x1, starting transfers between devices, local(): lax.all_to_all(stacked, 'feat', split_axis=0, concat_axis=2, tiled=True)[0]  4.24 us
    reduce_sum x1, other arithmetic, local(): centre_sq = jnp.sum(jnp.square(centres.astype(jnp.float32)), axis=1)  4.09 us
    scatter-add x1, other arithmetic, local(): jax.ops.segment_sum(jnp.ones_like(nearest), member, num_segments=centre_c...  3.39 us
  transfers between devices with their start and end apart: 2, of which 1 were waited for; matrix products, arithmetic and copies ran while one was open for 14% of the time, Pallas kernels for 0%

commit v1 on v0

--- a/solution.py
+++ b/solution.py
@@ -21,7 +21,32 @@
     size_part = jax.ops.segment_sum(jnp.ones_like(nearest), member, num_segments=centre_count)
     cluster_cost, cluster_size = lax.psum((cost_part, size_part), ("pts", "feat"))
     own_sens = nearest / jnp.take(cluster_cost, member) + 1.0 / jnp.take(cluster_size, member)
-    shard_sens = lax.all_gather(own_sens, "feat", axis=0, tiled=True)
+    tile_out = lax.axis_size("feat")
+    u1 = lax.axis_index("feat")
+    z, left_arr, a_now = (tile_out, u1, own_sens.shape[0])
+    row_list = []
+    for k, no in enumerate(own_sens.shape):
+        row_list.append(no * z if k == 0 else no)
+    shard_sens = lax.dynamic_update_slice_in_dim(
+        jnp.zeros(row_list, own_sens.dtype), own_sens, left_arr * a_now, axis=0
+    )
+    step_out = mixed_arr = own_sens
+    for nth in tuple(range(1, z // 2 + 1)):
+        panels = []
+        for k in [*range(z)]:
+            panels.append((k, (k + 1) % z))
+        step_out = lax.ppermute(step_out, "feat", perm=panels)
+        shard_sens = lax.dynamic_update_slice_in_dim(
+            shard_sens, step_out, (left_arr - nth) % z * a_now, axis=0
+        )
+        if 2 * nth < z:
+            by_rank = []
+            for k in tuple(range(z)):
+                by_rank.append((k, (k - 1) % z))
+            mixed_arr = lax.ppermute(mixed_arr, "feat", perm=by_rank)
+            shard_sens = lax.dynamic_update_slice_in_dim(
+                shard_sens, mixed_arr, (left_arr + nth) % z * a_now, axis=0
+            )
     total_points = rows_pts * lax.axis_size("pts")
     weight = 2.0 * centre_count / total_points / shard_sens
     picked_rows = sample_rows[0]

time: 100 us -> 99 us (0.990)
  blocking collectives: 47.4 us -> 41.7 us
  waiting for transfers between devices: 6.57 us -> 9.35 us
  starting transfers between devices: 9.3 us -> 11.4 us
    all_gather x1 -> x0, blocking collectives: 5.45 us -> none  [local(): shard_sens = lax.all_gather(own_sens, 'feat', axis=0, tiled=True)]
    ppermute x0 -> x3, waiting for transfers between devices: none -> 2.49 us  [the longest x2 2.49 us: local(): step_out = lax.ppermute(step_out, 'feat', perm=panels)]
    ppermute x0 -> x3, starting transfers between devices: none -> 1.8 us  [the longest x1 1.7 us: local(): mixed_arr = lax.ppermute(mixed_arr, 'feat', perm=by_rank)]
    unnamed x6 -> x8, local copies, waits for them, and re-layouts: 2.19 us -> 1.27 us
  transfers between devices with their start and end apart: 2 -> 5, of which waited for: 1 -> 4; matrix products, arithmetic and copies ran while one was open for 14% -> 13% of each run, Pallas kernels for 0% -> 0%
where the time goes in v1:
time: 99 us; the launch traced here: 98.5 us
  blocking collectives  41.7 us (42%)
  other arithmetic  16 us (16%)
  local copies, waits for them, and re-layouts  12.3 us (12%)
  starting transfers between devices  11.4 us (12%)
  waiting for transfers between devices  9.35 us (9%)
  matrix products  7.58 us (8%)
    psum x1, blocking collectives, local(): lax.psum((cost_part, size_part), ('pts', 'feat'))  41.7 us
    dot_general x1, matrix products, local(): lax.dot_general(points, centres, contract, preferred_element_type=jnp.flo...  7.58 us
    all_to_all x1, waiting for transfers between devices, local(): lax.all_to_all(scaled, 'pts', split_axis=0, concat_axis=0, tiled=True)  6.57 us
    all_to_all x1, starting transfers between devices, local(): lax.all_to_all(scaled, 'pts', split_axis=0, concat_axis=0, tiled=True)  5.33 us
    all_to_all x1, starting transfers between devices, local(): lax.all_to_all(stacked, 'feat', split_axis=0, concat_axis=2, tiled=True)[0]  4.24 us
    reduce_sum x1, other arithmetic, local(): centre_sq = jnp.sum(jnp.square(centres.astype(jnp.float32)), axis=1)  4.09 us
    scatter-add x1, other arithmetic, local(): jax.ops.segment_sum(jnp.ones_like(nearest), member, num_segments=centre_c...  3.39 us
    scatter-add x1, other arithmetic, local(): cost_part = jax.ops.segment_sum(nearest, member, num_segments=centre_count)  3.26 us
  transfers between devices with their start and end apart: 5, of which 4 were waited for; matrix products, arithmetic and copies ran while one was open for 13% of the time, Pallas kernels for 0%

profile of v1, /device:TPU:0, one launch (start us, length us, event | category | flops | bytes accessed | tf_op | source)
XLA Modules:
  0.0 98.5 jit_solution(893397196803037768)
XLA Ops:
  0.0 2.1 %copy.35 = bf16[24,4,8,512]{3,2,0,1:T(8,128)(2,1)} copy(bf16[24,4,8,512]{3,2,1,0:T(8,128)(2,1)} %bitcast.28) | data formatting | bytes 1572864 | tf_op jit(solution)/shard_map/reshape | solution.py:14
  2.1 4.2 %all-to-all-start = ((bf16[4,512,192]{1,2,0:T(8,128)(2,1)}), bf16[4,512,192]{1,2,0:T(8,128)(2,1)S(1)}, u32[]{:S(2)}, u32[]{:S(2)}) async-start(bf16[4,512,192]{1,2,0:T(8,128)(2,1)} %bitcast.27), calls=%async_computation | async-start | bytes 1572864 | tf_op jit(solution)/shard_map/all_to_all | solution.py:15
  6.3 0.7 compare_select_fusion.1
  7.0 0.8 copy.27
  7.8 0.7 compare_select_fusion
  8.7 0.7 iota_compare_fusion
  9.4 0.7 iota_add_fusion
  10.2 3.4 %scatter_custom_fusion.1 = f32[4096]{0:T(1024)S(1)} fusion(s32[512]{0:T(512)} %bitcast.31, f32[512]{0:T(512)S(1)} %broadcast.116, f32[]{:T(128)} %constant.48.clone.1), kind=kCustom, calls=%fused_computation.14 | custom fusion | flops 512 | bytes 16896 | tf_op jit(solution)/shard_map/scatter-add | solution.py:21
  13.6 4.1 %multiply_reduce_fusion = f32[4096]{0:T(1024)S(1)} fusion(bf16[4096,768]{1,0:T(8,128)(2,1)} %param.9), kind=kLoop, calls=%fused_computation.7 | loop fusion | flops 9433088 | bytes 6307840 | tf_op jit(solution)/shard_map/reduce_sum | solution.py:13
  18.2 7.6 %subtract_reduce_fusion = f32[512]{0:T(512)S(1)} fusion(bf16[512,768]{0,1:T(8,128)(2,1)S(1)} %bitcast.29, bf16[4096,768]{1,0:T(8,128)(2,1)} %param.9, f32[4096]{0:T(1024)S(1)} %multiply_reduce_fusion, f32[512]{0:T(512)S(1)} %multiply_reduce_fusion.1), kind=kOutput, calls=%fused_computation.8 | convolution fusion | flops 3229613568 | bytes 7098368 | tf_op jit(solution)/shard_map/dot_general | solution.py:16
  25.8 3.3 %scatter_custom_fusion = f32[4096]{0:T(1024)S(1)} fusion(s32[512]{0:T(512)S(1)} %bitcast.32, f32[512]{0:T(512)S(1)} %subtract_reduce_fusion, f32[]{:T(128)} %constant.48.clone.1), kind=kCustom, calls=%fused_computation.16 | custom fusion | flops 512 | bytes 16388 | tf_op jit(solution)/shard_map/scatter-add | solution.py:20
  29.0 41.7 %all-reduce = (f32[4096]{0:T(1024)S(1)}, f32[4096]{0:T(1024)S(1)}) all-reduce(f32[4096]{0:T(1024)S(1)} %scatter_custom_fusion.1, f32[4096]{0:T(1024)S(1)} %scatter_custom_fusion), channel_id=1, replica_groups=mesh['pts'=8,'feat'=4] {'pts','feat'}, use_global_device_ids=true, to_apply=%region_6.8 | all-reduce | flops 8192 | bytes 65536 | tf_op jit(solution)/shard_map/psum | solution.py:22
  70.8 3.1 %gather_fusion.2 = f32[512]{0:T(512)S(1)} fusion(f32[4096]{0:T(1024)S(1)} %get-tuple-element.7, s32[1024]{0:T(1024)S(1)} %pad_clamp_fusion.1), kind=kCustom, calls=%fused_computation.clone | custom fusion | bytes 6144 | tf_op jit(solution)/shard_map/jit(_take)/gather | solution.py:23
  73.9 3.1 %gather_fusion.3 = f32[512]{0:T(512)S(1)} fusion(f32[4096]{0:T(1024)S(1)} %get-tuple-element.6, s32[1024]{0:T(1024)S(1)} %pad_clamp_fusion.1), kind=kCustom, calls=%fused_computation.1.clone | custom fusion | bytes 6144 | tf_op jit(solution)/shard_map/jit(_take)/gather | solution.py:23
  77.3 1.7 %collective-permute-start.1 = (f32[512]{0:T(512)S(1)}, f32[512]{0:T(512)S(1)}, u32[]{:S(2)}, u32[]{:S(2)}) collective-permute-start(f32[512]{0:T(512)S(1)} %get-tuple-element.11), channel_id=1, source_target_pairs={{0,3},{1,0},{2,1},{3,2},{4,7},{5,4},{6,5},{7,6},{8,11},{9,8},{10,9... | collective-permute-start | bytes 6152 | tf_op jit(solution)/shard_map/ppermute | solution.py:46
  79.0 1.3 %collective-permute-done = f32[512]{0:T(512)S(1)} collective-permute-done((f32[512]{0:T(512)S(1)}, f32[512]{0:T(512)S(1)}, u32[]{:S(2)}, u32[]{:S(2)}) %collective-permute-start) | collective-permute-done | bytes 2080 | tf_op jit(solution)/shard_map/ppermute | solution.py:38
  80.8 0.6 gather_fusion
  82.0 1.2 %collective-permute-done.2 = f32[512]{0:T(512)S(1)} collective-permute-done((f32[512]{0:T(512)S(1)}, f32[512]{0:T(512)S(1)}, u32[]{:S(2)}, u32[]{:S(2)}) %collective-permute-start.2) | collective-permute-done | bytes 2080 | tf_op jit(solution)/shard_map/ppermute | solution.py:38
  83.4 0.7 gather_fusion.1
  84.5 0.7 select_convert_fusion
  85.2 5.3 %all-to-all-start.1 = ((bf16[8,4,192]{2,1,0:T(4,128)(2,1)}), bf16[8,4,192]{2,1,0:T(4,128)(2,1)S(1)}, u32[]{:S(2)}, u32[]{:S(2)}) async-start(bf16[8,4,192]{2,1,0:T(4,128)(2,1)} %select_convert_fusion), calls=%async_computation.1 | async-start | bytes 32768 | tf_op jit(solution)/shard_map/all_to_all | solution.py:62
  90.5 6.6 %all-to-all-done.1 = bf16[8,4,192]{2,1,0:T(4,128)(2,1)S(1)} async-done(((bf16[8,4,192]{2,1,0:T(4,128)(2,1)}), bf16[8,4,192]{2,1,0:T(4,128)(2,1)S(1)}, u32[]{:S(2)}, u32[]{:S(2)}) %all-to-all-start.1) | async-done | bytes 12320 | tf_op jit(solution)/shard_map/all_to_all | solution.py:62
  97.1 0.8 scatter_custom_fusion.2
  97.9 0.6 convert_element_type.28
  (35 shorter events, 2.6 us)
Async XLA Ops:
  2.1 15.9 %all-to-all-start = ((bf16[4,512,192]{1,2,0:T(8,128)(2,1)}), bf16[4,512,192]{1,2,0:T(8,128)(2,1)S(1)}, u32[]{:S(2)}, u32[]{:S(2)}) async-start(bf16[4,512,192]{1,2,0:T(8,128)(2,1)} %bitcast.27), calls=%async_computation | async-start | bytes 1572864 | tf_op jit(solution)/shard_map/all_to_all | solution.py:15
  18.2 7.6 %copy-start.2 = (s32[512,1]{0,1:T(1,128)S(1)}, s32[512,1]{0,1:T(1,128)}, u32[]{:S(2)}) copy-start(s32[512,1]{0,1:T(1,128)} %param.10) | copy-start | bytes 6148
  18.2 62.2 %copy-start = (bf16[2048,192]{0,1:T(8,128)(2,1)S(1)}, bf16[2048,192]{0,1:T(8,128)(2,1)}, u32[]{:S(2)}) copy-start(bf16[2048,192]{0,1:T(8,128)(2,1)} %param.8) | copy-start | bytes 2359300
  25.8 58.5 %copy-start.1 = (s32[1,8,4]{1,2,0:T(4,128)S(1)}, s32[1,8,4]{1,2,0:T(4,128)}, u32[]{:S(2)}) copy-start(s32[1,8,4]{1,2,0:T(4,128)} %param.11) | copy-start | bytes 388
  77.2 3.0 %collective-permute-start = (f32[512]{0:T(512)S(1)}, f32[512]{0:T(512)S(1)}, u32[]{:S(2)}, u32[]{:S(2)}) collective-permute-start(f32[512]{0:T(512)S(1)} %get-tuple-element.11), channel_id=1, source_target_pairs={{0,1},{1,2},{2,3},{3,0},{4,5},{5,6},{6,7},{7,4},{8,9},{9,10},{10,1... | collective-permute-start | bytes 6152 | tf_op jit(solution)/shard_map/ppermute | solution.py:38
  77.3 4.5 %collective-permute-start.1 = (f32[512]{0:T(512)S(1)}, f32[512]{0:T(512)S(1)}, u32[]{:S(2)}, u32[]{:S(2)}) collective-permute-start(f32[512]{0:T(512)S(1)} %get-tuple-element.11), channel_id=1, source_target_pairs={{0,3},{1,0},{2,1},{3,2},{4,7},{5,4},{6,5},{7,6},{8,11},{9,8},{10,9... | collective-permute-start | bytes 6152 | tf_op jit(solution)/shard_map/ppermute | solution.py:46
  80.2 3.0 %collective-permute-start.2 = (f32[512]{0:T(512)S(1)}, f32[512]{0:T(512)S(1)}, u32[]{:S(2)}, u32[]{:S(2)}) collective-permute-start(f32[512]{0:T(512)S(1)} %collective-permute-done), channel_id=1, source_target_pairs={{0,1},{1,2},{2,3},{3,0},{4,5},{5,6},{6,7},{7,4},{8,9},{9,10},{10,1... | collective-permute-start | bytes 6152 | tf_op jit(solution)/shard_map/ppermute | solution.py:38
  85.2 11.9 %all-to-all-start.1 = ((bf16[8,4,192]{2,1,0:T(4,128)(2,1)}), bf16[8,4,192]{2,1,0:T(4,128)(2,1)S(1)}, u32[]{:S(2)}, u32[]{:S(2)}) async-start(bf16[8,4,192]{2,1,0:T(4,128)(2,1)} %select_convert_fusion), calls=%async_computation.1 | async-start | bytes 32768 | tf_op jit(solution)/shard_map/all_to_all | solution.py:62
